TPU v7x, 32 devices: a whole 2x2x4 slice. The times are simulated.
32 devices in a mesh: groups: 2 (over y), expert: 4 (over x, core), hidden: 4 (over z).
Axes of the slice: x: 2, y: 2, z: 4, core: 2. Of those that a mesh axis runs over, the one named last changes fastest.
Arguments:
- tokens: bfloat16 [1024, 3072], P(('groups', 'expert'), 'hidden'), parts along dimension 0, may hold values from -6 to 6
- routes: int32 [1024, 2], P(('groups', 'expert')), parts along dimension 0, may hold values from 0 to 7, all different within a row; in each aligned block of 128 rows (0 to 127, 128 to 255, ...) at most 48 rows name the same one
- router_weight: bfloat16 [3072, 8], replicated, may hold values from -0.109375 to 0.109375
- gate_weight: bfloat16 [8, 3072, 8192], P('expert', None, 'hidden'), may hold values from -0.109375 to 0.109375
- up_weight: bfloat16 [8, 3072, 8192], P('expert', None, 'hidden'), may hold values from -0.109375 to 0.109375
- down_weight: bfloat16 [8, 8192, 3072], P('expert', 'hidden'), may hold values from -0.09375 to 0.09375
Outputs:
- mixed: bfloat16 [1024, 3072], P(('groups', 'expert'), 'hidden'), parts along dimension 0
There are 2 independent parts, one for each index of `groups`. A program takes and returns all parts, laid end to end along the dimension named above; an argument that names none is the same for every part. Nothing has to cross between parts.
Inputs may be any that keep to these rules, and one draw needn't show every extreme that they name: `routes`: each token names two different experts. Among the 128 tokens of one index of expert (aligned blocks of rows) no expert is named more than 48 times, a bound that some block reaches.
All inputs are finite; a program needn't handle non-finite values.
Results may differ from a plain program's by a relative error of at most 0.0057.
Values may be sent and summed in bfloat16 or wider, within the bound.
No kernel may reach another device: no remote copies, remote signals or barrier semaphores. Data moves between devices by JAX's collectives and lax.ppermute only.
A program may use at most 128 MiB of HBM per device.

v0:
```python
import jax
import jax.numpy as jnp
from jax import lax
from jax.sharding import PartitionSpec as P

CAP = 48


def per_device(tokens, routes, router_weight, gate_weight, up_weight, down_weight):
    experts_here = gate_weight.shape[0]
    groups = lax.axis_size("expert")
    experts_all = experts_here * groups
    local_tokens = tokens.shape[0]
    capacity = CAP
    flat_ids = routes.reshape(-1)
    onehot = (flat_ids[:, None] == jnp.arange(experts_all, dtype=jnp.int32)[None, :]).astype(
        jnp.int32
    )
    position = jnp.sum((jnp.cumsum(onehot, axis=0) - onehot) * onehot, axis=1)
    slot_of = flat_ids * capacity + position
    owners = jnp.arange(flat_ids.shape[0], dtype=jnp.int32) // 2
    inverse = jnp.full((experts_all * capacity,), local_tokens, jnp.int32).at[slot_of].set(owners)
    gathered = lax.all_gather(tokens, "hidden", axis=1, tiled=True)
    logits = jnp.dot(gathered, router_weight, preferred_element_type=jnp.float32)
    padded = jnp.concatenate([gathered, jnp.zeros((1, gathered.shape[1]), jnp.bfloat16)], axis=0)
    send_rows = padded[inverse].reshape(experts_all, 1, capacity, gathered.shape[1])
    arrived = lax.all_to_all(send_rows, "expert", split_axis=0, concat_axis=1, tiled=True)
    gate_act = jnp.einsum(
        "ensd,edf->ensf", arrived, gate_weight, preferred_element_type=jnp.float32
    )
    up_act = jnp.einsum("ensd,edf->ensf", arrived, up_weight, preferred_element_type=jnp.float32)
    hidden_act = (jax.nn.silu(gate_act) * up_act).astype(jnp.bfloat16)
    hidden_act = hidden_act.reshape(experts_here, groups * capacity, hidden_act.shape[3])
    partial_value = jnp.einsum(
        "erf,efd->erd", hidden_act, down_weight, preferred_element_type=jnp.float32
    )
    summed = lax.psum_scatter(partial_value, "hidden", scatter_dimension=2, tiled=True).astype(
        jnp.bfloat16
    )
    summed = summed.reshape(experts_here, groups, capacity, summed.shape[2])
    returned = lax.all_to_all(summed, "expert", split_axis=1, concat_axis=0, tiled=True)
    results = returned.reshape(experts_all * capacity, returned.shape[3])
    selected = jnp.take_along_axis(logits, routes, axis=1)
    share = jax.nn.sigmoid(selected[:, 0] - selected[:, 1])
    slot_pairs = slot_of.reshape(local_tokens, 2)
    first_out = results[slot_pairs[:, 0]].astype(jnp.float32)
    second_out = results[slot_pairs[:, 1]].astype(jnp.float32)
    mixture = share[:, None] * first_out + (1.0 - share)[:, None] * second_out
    return mixture.astype(jnp.bfloat16)


def solution(mesh):
    return jax.shard_map(
        per_device,
        mesh=mesh,
        in_specs=(
            P(("groups", "expert"), "hidden"),
            P(("groups", "expert"), None),
            P(),
            P("expert", None, "hidden"),
            P("expert", None, "hidden"),
            P("expert", "hidden", None),
        ),
        out_specs=P(("groups", "expert"), "hidden"),
        check_vma=False,
    )
```

profile of v0, /device:TPU:0, one launch (start us, length us, event | category | flops | bytes accessed | tf_op | source)
XLA Modules:
  0.0 209.8 jit_solution(10546477326377145028)
XLA Ops:
  6.5 0.8 copy.41
  7.6 0.6 reduce-window.6
  8.2 0.2 slice_reduce_fusion
  8.9 1.4 scatter_custom_fusion
  10.3 21.5 %all_gather.3 = bf16[128,3072]{1,0:T(8,128)(2,1)S(1)} all-gather(bf16[128,768]{1,0:T(8,128)(2,1)} %param.6), channel_id=1, replica_groups=mesh['groups'=2,'expert'=4,'hidden'=4] {'hidden'}, dimensions={1}, use_global_device_ids=true | all-gather | bytes 983040 | tf_op jit(solution)/shard_map/all_gather | solution.py:23
  31.8 0.9 copy-done.1
  32.8 2.9 %gather_fusion = bf16[384,3072]{1,0:T(8,128)(2,1)S(1)} fusion(bf16[129,3072]{1,0:T(8,128)(2,1)S(1)} %concatenate.3, s32[1024]{0:T(1024)S(1)} %pad_clamp_fusion.2), kind=kCustom, calls=%fused_computation | custom fusion | bytes 4720128 | tf_op jit(solution)/shard_map/gather | solution.py:26
  35.7 31.0 %all_to_all.33 = bf16[8,1,48,3072]{3,2,1,0:T(8,128)(2,1)S(1)} all-to-all(bf16[8,1,48,3072]{3,2,1,0:T(8,128)(2,1)S(1)} %bitcast.57), channel_id=1, replica_groups=mesh['groups'=2,'expert'=4,'hidden'=4] {'expert'}, dimensions={0} | all-to-all | bytes 4718592 | tf_op jit(solution)/shard_map/all_to_all | solution.py:27
  66.7 10.8 %fusion.2 = f32[2,4,48,2048]{3,2,1,0:T(8,128)S(1)} fusion(bf16[2,3072,2048]{2,1,0:T(8,128)(2,1)} %param.9, bf16[4,2,1,48,3072]{4,3,1,0,2:T(8,128)(2,1)S(1)} %bitcast.52), kind=kOutput, calls=%fused_computation.7 | convolution fusion | flops 4831838208 | bytes 30670848 | tf_op jit(solution)/shard_map/ensd,edf->ensf/dot_general | solution.py:28
  77.5 11.0 %multiply_convert_fusion = bf16[2,4,48,2048]{3,2,1,0:T(8,128)(2,1)S(1)} fusion(f32[2,4,48,2048]{3,2,1,0:T(8,128)S(1)} %fusion.2, bf16[2,3072,2048]{2,1,0:T(8,128)(2,1)} %param.10, bf16[4,2,1,48,3072]{4,3,1,0,2:T(8,128)(2,1)S(1)} %bitcast.53), kind=kOutput, calls=%fused_computation.9 | convolution fusion | flops 4836556800 | bytes 32243712 | tf_op jit(solution)/shard_map/ensd,edf->ensf/dot_general | solution.py:31
  88.5 12.9 %fusion.19 = f32[2,192,3072]{2,1,0:T(8,128)} fusion(bf16[2,192,2048]{2,1,0:T(8,128)(2,1)S(1)} %bitcast.56, bf16[2,2048,3072]{2,1,0:T(8,128)(2,1)} %param.11), kind=kOutput, calls=%fused_computation.45 | convolution fusion | flops 4831838208 | bytes 31457280 | tf_op jit(solution)/shard_map/erf,efd->erd/dot_general | solution.py:34
  101.5 0.7 copy-done.3
  102.4 0.2 copy-done.2
  102.6 0.3 fusion.18
  102.9 1.4 gather_fusion.3
  104.5 0.2 fusion.10
  104.7 80.6 %reduce-scatter.2.cloned.1.call-done = f32[2,192,768]{2,1,0:T(8,128)} async-done(((f32[2,192,3072]{2,1,0:T(8,128)}), f32[2,192,768]{2,1,0:T(8,128)}) %reduce-scatter.2.cloned.1.call-update) | async-done | bytes 1179664 | tf_op jit(solution)/shard_map/reduce_scatter | solution.py:37
  185.3 1.3 convert_element_type.25
  186.6 0.8 copy.46
  187.5 3.5 %all-to-all-start.1 = ((bf16[2,4,48,768]{3,2,0,1:T(8,128)(2,1)}), bf16[2,4,48,768]{3,2,0,1:T(8,128)(2,1)S(1)}, u32[]{:S(2)}, u32[]{:S(2)}) async-start(bf16[2,4,48,768]{3,2,0,1:T(8,128)(2,1)} %copy.46), calls=%async_computation.2 | async-start | bytes 1179648 | tf_op jit(solution)/shard_map/all_to_all | solution.py:41
  191.0 9.5 %all-to-all-done.1 = bf16[2,4,48,768]{3,2,0,1:T(8,128)(2,1)S(1)} async-done(((bf16[2,4,48,768]{3,2,0,1:T(8,128)(2,1)}), bf16[2,4,48,768]{3,2,0,1:T(8,128)(2,1)S(1)}, u32[]{:S(2)}, u32[]{:S(2)}) %all-to-all-start.1) | async-done | bytes 589856 | tf_op jit(solution)/shard_map/all_to_all | solution.py:41
  200.4 0.9 gather_fusion.2
  201.3 0.9 gather_fusion.1
  202.2 0.8 add_convert_fusion
  (29 shorter events, 1.3 us)
Async XLA Ops:
  6.5 95.8 %copy-start = (bf16[3072,8]{0,1:T(8,128)(2,1)S(1)}, bf16[3072,8]{0,1:T(8,128)(2,1)}, u32[]{:S(2)}) copy-start(bf16[3072,8]{0,1:T(8,128)(2,1)} %param.8) | copy-start | bytes 147460
  6.5 178.8 %reduce-scatter.2.cloned.1.call-start = ((), (), s32[]{:S(2)}) async-start(), calls=%async_computation.3 | async-start | bytes 5898240 | tf_op jit(solution)/shard_map/reduce_scatter | solution.py:37
  31.8 0.9 copy-start.1
  101.4 0.7 copy-start.3
  101.4 1.1 copy-start.2
  187.5 13.0 %all-to-all-start.1 = ((bf16[2,4,48,768]{3,2,0,1:T(8,128)(2,1)}), bf16[2,4,48,768]{3,2,0,1:T(8,128)(2,1)S(1)}, u32[]{:S(2)}, u32[]{:S(2)}) async-start(bf16[2,4,48,768]{3,2,0,1:T(8,128)(2,1)} %copy.46), calls=%async_computation.2 | async-start | bytes 1179648 | tf_op jit(solution)/shard_map/all_to_all | solution.py:41
Sparse Core Ops, SparseCore 0:
  101.6 83.6 reduce-scatter.1
where the time goes:
time: 210 us
  waiting for transfers between devices  90.1 us (43%)
  blocking collectives  52.6 us (25%)
  matrix products  35 us (17%)
  between operations  13.6 us (6%)
  local copies, waits for them, and re-layouts  12.1 us (6%)
  starting transfers between devices  3.48 us (2%)
  other arithmetic  3.13 us (1%)
    reduce_scatter x1, waiting for transfers between devices, per_device(): lax.psum_scatter(partial_value, 'hidden', scatter_dimension=2, tiled=True)  80.6 us
    all_to_all x1, blocking collectives, per_device(): lax.all_to_all(send_rows, 'expert', split_axis=0, concat_axis=1, tiled=True)  31 us
    all_gather x1, blocking collectives, per_device(): gathered = lax.all_gather(tokens, 'hidden', axis=1, tiled=True)  21.5 us
    dot_general x1, matrix products, per_device(): jnp.einsum('erf,efd->erd', hidden_act, down_weight, preferred_element_typ...  12.9 us
    dot_general x1, matrix products, per_device(): jnp.einsum('ensd,edf->ensf', arrived, up_weight, preferred_element_type=j...  11 us
    dot_general x1, matrix products, per_device(): jnp.einsum('ensd,edf->ensf', arrived, gate_weight, preferred_element_type...  10.8 us
    all_to_all x1, waiting for transfers between devices, per_device(): lax.all_to_all(summed, 'expert', split_axis=1, concat_axis=0, tiled=True)  9.45 us
  transfers between devices with their start and end apart: 2, of which 2 were waited for; matrix products, arithmetic and copies ran while one was open for 1% of the time, Pallas kernels for 0%

commit v1 on v0

--- a/solution.py
+++ b/solution.py
@@ -24,7 +24,12 @@
     logits = jnp.dot(gathered, router_weight, preferred_element_type=jnp.float32)
     padded = jnp.concatenate([gathered, jnp.zeros((1, gathered.shape[1]), jnp.bfloat16)], axis=0)
     send_rows = padded[inverse].reshape(experts_all, 1, capacity, gathered.shape[1])
-    arrived = lax.all_to_all(send_rows, "expert", split_axis=0, concat_axis=1, tiled=True)
+    arrived = jnp.concatenate(
+        lax.all_to_all(
+            jnp.stack(jnp.split(send_rows, lax.axis_size("expert"), axis=0)), "expert", 0, 0
+        ),
+        axis=1,
+    )
     gate_act = jnp.einsum(
         "ensd,edf->ensf", arrived, gate_weight, preferred_element_type=jnp.float32
     )

time: 210 us -> 211 us (level)
  no operation moved by 1% of the time
where the time goes in v1:
time: 211 us; the launch traced here: 210 us
  waiting for transfers between devices  90.1 us (43%)
  blocking collectives  52.6 us (25%)
  matrix products  35 us (17%)
  between operations  13.6 us (6%)
  local copies, waits for them, and re-layouts  12.2 us (6%)
  starting transfers between devices  3.48 us (2%)
  other arithmetic  3.42 us (2%)
    reduce_scatter x1, waiting for transfers between devices, per_device(): lax.psum_scatter(partial_value, 'hidden', scatter_dimension=2, tiled=True)  80.6 us
    all_to_all x1, blocking collectives, per_device(): lax.all_to_all(jnp.stack(jnp.split(send_rows, lax.axis_size('expert'), ax...  31 us
    all_gather x1, blocking collectives, per_device(): gathered = lax.all_gather(tokens, 'hidden', axis=1, tiled=True)  21.5 us
    dot_general x1, matrix products, per_device(): jnp.einsum('erf,efd->erd', hidden_act, down_weight, preferred_element_typ...  12.9 us
    dot_general x1, matrix products, per_device(): jnp.einsum('ensd,edf->ensf', arrived, up_weight, preferred_element_type=j...  10.9 us
    dot_general x1, matrix products, per_device(): jnp.einsum('ensd,edf->ensf', arrived, gate_weight, preferred_element_type...  10.8 us
    all_to_all x1, waiting for transfers between devices, per_device(): lax.all_to_all(summed, 'expert', split_axis=1, concat_axis=0, tiled=True)  9.45 us
  transfers between devices with their start and end apart: 2, of which 2 were waited for; matrix products, arithmetic and copies ran while one was open for 1% of the time, Pallas kernels for 0%

profile of v1, /device:TPU:0, one launch (start us, length us, event | category | flops | bytes accessed | tf_op | source)
XLA Modules:
  0.0 210.3 jit_solution(3298297296818344044)
XLA Ops:
  6.5 0.8 copy.38
  7.6 0.6 reduce-window.6
  8.2 0.2 slice_reduce_fusion
  8.9 1.4 scatter_custom_fusion
  10.3 21.5 %all_gather.3 = bf16[128,3072]{1,0:T(8,128)(2,1)S(1)} all-gather(bf16[128,768]{1,0:T(8,128)(2,1)} %param.6), channel_id=1, replica_groups=mesh['groups'=2,'expert'=4,'hidden'=4] {'hidden'}, dimensions={1}, use_global_device_ids=true | all-gather | bytes 983040 | tf_op jit(solution)/shard_map/all_gather | solution.py:23
  31.8 0.9 copy-done.1
  32.8 2.9 %gather_fusion = bf16[384,3072]{1,0:T(8,128)(2,1)S(1)} fusion(bf16[129,3072]{1,0:T(8,128)(2,1)S(1)} %concatenate.3, s32[1024]{0:T(1024)S(1)} %pad_clamp_fusion.2), kind=kCustom, calls=%fused_computation | custom fusion | bytes 4720128 | tf_op jit(solution)/shard_map/gather | solution.py:26
  35.9 0.3 pad_maximum_fusion
  36.2 31.0 %all_to_all.20 = bf16[4,2,1,48,3072]{4,3,1,2,0:T(8,128)(2,1)S(1)} all-to-all(bf16[4,2,1,48,3072]{4,3,1,2,0:T(8,128)(2,1)S(1)} %pad_maximum_fusion), channel_id=1, replica_groups=mesh['groups'=2,'expert'=4,'hidden'=4] {'expert'}, dimensions={0} | all-to-all | bytes 4718592 | tf_op jit(solution)/shard_map/all_to_all | solution.py:28
  67.2 10.8 %fusion.2 = f32[2,4,48,2048]{3,2,1,0:T(8,128)S(1)} fusion(bf16[2,3072,2048]{2,1,0:T(8,128)(2,1)} %param.9, bf16[4,2,1,48,3072]{4,3,1,2,0:T(8,128)(2,1)S(1)} %all_to_all.20), kind=kOutput, calls=%fused_computation.7 | convolution fusion | flops 4831838208 | bytes 30670848 | tf_op jit(solution)/shard_map/ensd,edf->ensf/dot_general | solution.py:33
  78.0 10.9 %multiply_convert_fusion = bf16[2,4,48,2048]{3,2,1,0:T(8,128)(2,1)S(1)} fusion(f32[2,4,48,2048]{3,2,1,0:T(8,128)S(1)} %fusion.2, bf16[2,3072,2048]{2,1,0:T(8,128)(2,1)} %param.10, bf16[4,2,1,48,3072]{4,3,1,2,0:T(8,128)(2,1)S(1)} %all_to_all.20), kind=kOutput, calls=%fused_computation.9 | convolution fusion | flops 4836556800 | bytes 32243712 | tf_op jit(solution)/shard_map/ensd,edf->ensf/dot_general | solution.py:36
  88.9 12.9 %fusion.20 = f32[2,192,3072]{2,1,0:T(8,128)} fusion(bf16[2,192,2048]{2,1,0:T(8,128)(2,1)S(1)} %bitcast.54, bf16[2,2048,3072]{2,1,0:T(8,128)(2,1)} %param.11), kind=kOutput, calls=%fused_computation.47 | convolution fusion | flops 4831838208 | bytes 31457280 | tf_op jit(solution)/shard_map/erf,efd->erd/dot_general | solution.py:39
  101.9 0.7 copy-done.3
  103.0 0.3 fusion.19
  103.3 1.4 gather_fusion.3
  104.9 0.2 fusion.10
  105.1 80.6 %reduce-scatter.2.cloned.1.call-done = f32[2,192,768]{2,1,0:T(8,128)} async-done(((f32[2,192,3072]{2,1,0:T(8,128)}), f32[2,192,768]{2,1,0:T(8,128)}) %reduce-scatter.2.cloned.1.call-update) | async-done | bytes 1179664 | tf_op jit(solution)/shard_map/reduce_scatter | solution.py:42
  185.8 1.3 convert_element_type.25
  187.1 0.8 copy.42
  188.0 3.5 %all-to-all-start.1 = ((bf16[2,4,48,768]{3,2,0,1:T(8,128)(2,1)}), bf16[2,4,48,768]{3,2,0,1:T(8,128)(2,1)S(1)}, u32[]{:S(2)}, u32[]{:S(2)}) async-start(bf16[2,4,48,768]{3,2,0,1:T(8,128)(2,1)} %copy.42), calls=%async_computation.2 | async-start | bytes 1179648 | tf_op jit(solution)/shard_map/all_to_all | solution.py:46
  191.5 9.5 %all-to-all-done.1 = bf16[2,4,48,768]{3,2,0,1:T(8,128)(2,1)S(1)} async-done(((bf16[2,4,48,768]{3,2,0,1:T(8,128)(2,1)}), bf16[2,4,48,768]{3,2,0,1:T(8,128)(2,1)S(1)}, u32[]{:S(2)}, u32[]{:S(2)}) %all-to-all-start.1) | async-done | bytes 589856 | tf_op jit(solution)/shard_map/all_to_all | solution.py:46
  200.9 0.9 gather_fusion.2
  201.8 0.9 gather_fusion.1
  202.7 0.8 add_convert_fusion
  (31 shorter events, 1.6 us)
Async XLA Ops:
  6.5 96.3 %copy-start = (bf16[3072,8]{0,1:T(8,128)(2,1)S(1)}, bf16[3072,8]{0,1:T(8,128)(2,1)}, u32[]{:S(2)}) copy-start(bf16[3072,8]{0,1:T(8,128)(2,1)} %param.8) | copy-start | bytes 147460
  6.5 179.2 %reduce-scatter.2.cloned.1.call-start = ((), (), s32[]{:S(2)}) async-start(), calls=%async_computation.3 | async-start | bytes 5898240 | tf_op jit(solution)/shard_map/reduce_scatter | solution.py:42
  31.8 0.9 copy-start.1
  101.9 0.7 copy-start.3
  101.9 1.1 copy-start.2
  188.0 13.0 %all-to-all-start.1 = ((bf16[2,4,48,768]{3,2,0,1:T(8,128)(2,1)}), bf16[2,4,48,768]{3,2,0,1:T(8,128)(2,1)S(1)}, u32[]{:S(2)}, u32[]{:S(2)}) async-start(bf16[2,4,48,768]{3,2,0,1:T(8,128)(2,1)} %copy.42), calls=%async_computation.2 | async-start | bytes 1179648 | tf_op jit(solution)/shard_map/all_to_all | solution.py:46
Sparse Core Ops, SparseCore 0:
  102.0 83.6 reduce-scatter.1
